TPU v7x, 512 devices: a whole 4x8x8 slice. The times are simulated.
512 devices in a mesh: rec: 8 (over x, y_hi), row: 4 (over y_lo), col: 16 (over z, core).
Axes of the slice: x: 4, y: 8 (y_hi: 2, y_lo: 4; y = y_hi * 4 + y_lo), z: 8, core: 2. Of those that a mesh axis runs over, the one named last changes fastest.
Arguments:
- local_derivs: bfloat16 [1024, 256, 128], P(('rec', 'row', 'col')), may hold values from -6 to 6
- global_derivs: bfloat16 [1024, 256, 384], P(('rec', 'row', 'col')), may hold values from -64 to 64
- weights: float32 [1024, 256], P(('rec', 'row', 'col')), may hold values from 0.25 to 4
- first_block: int32 [1024], P(('rec', 'row', 'col')), may hold values from 0 to 6
- bundle_count: int32 [512], P(('rec', 'row', 'col')), may hold values from 1 to 2
- trailing_block: float32 [8192, 8192], P(('rec', 'row'), 'col'), may hold values from -6 to 6
Outputs:
- updated: float32 [8192, 8192], P(('rec', 'row'), 'col')
All inputs are finite; a program needn't handle non-finite values.
Results may differ from a plain program's by a relative error of at most 0.0094.
Values may be sent and summed in bfloat16 or wider, within the bound.
A program may use at most 64 MiB of HBM per device.

v0:
```python
import jax
import jax.numpy as jnp
from jax import lax
from jax.sharding import PartitionSpec as P

PBLK = 8


HIGH = lax.Precision.HIGHEST


def shifted(shard, axis, by):
    length = lax.axis_size(axis)
    pairs = [(i, i + by) for i in range(length) if 0 <= i + by < length]
    return lax.ppermute(shard, axis, pairs)


def invert_lower(factor):
    eye = jnp.eye(factor.shape[-1], dtype=factor.dtype)
    eye = jnp.broadcast_to(eye, factor.shape)
    return lax.linalg.triangular_solve(factor, eye, left_side=True, lower=True)


def bundle_terms(local_derivs, global_derivs, weights, first_block, live, panel_blocks):
    block = global_derivs.shape[2] // 3
    root = jnp.sqrt(weights)[:, :, None]
    scaled_local = (root * local_derivs.astype(jnp.float32)).astype(jnp.bfloat16)
    scaled_global = (root * global_derivs.astype(jnp.float32)).astype(jnp.bfloat16)
    local_gram = jnp.einsum(
        "nrl,nrm->nlm", scaled_local, scaled_local, preferred_element_type=jnp.float32
    )
    cross_gram = jnp.einsum(
        "nrg,nrl->ngl", scaled_global, scaled_local, preferred_element_type=jnp.float32
    )
    panel_gram = jnp.einsum(
        "nra,nrg->nag",
        scaled_global[:, :, : 2 * block],
        scaled_global,
        preferred_element_type=jnp.float32,
    )
    local_inverse = invert_lower(jnp.linalg.cholesky(local_gram))
    whitened = jnp.einsum("nlm,ngm->nlg", local_inverse, cross_gram, precision=HIGH)
    reduced = panel_gram - jnp.einsum(
        "nla,nlg->nag", whitened[:, :, : 2 * block], whitened, precision=HIGH
    )
    reduced = reduced * live[:, None, None]
    marks = jnp.arange(panel_blocks, dtype=jnp.int32)
    first_hot = (first_block[:, None] == marks[None, :]).astype(jnp.float32)
    second_hot = (first_block[:, None] + 1 == marks[None, :]).astype(jnp.float32)
    diag_part = jnp.einsum("nk,nab->kab", first_hot, reduced[:, :block, :block], precision=HIGH)
    diag_part = diag_part + jnp.einsum(
        "nk,nab->kab", second_hot, reduced[:, block : 2 * block, block : 2 * block], precision=HIGH
    )
    sub_part = jnp.einsum(
        "nk,nab->kab", second_hot, reduced[:, block : 2 * block, :block], precision=HIGH
    )
    panel_part = jnp.einsum(
        "nk,nab->kab", first_hot, reduced[:, :block, 2 * block :], precision=HIGH
    )
    panel_part = panel_part + jnp.einsum(
        "nk,nab->kab", second_hot, reduced[:, block : 2 * block, 2 * block :], precision=HIGH
    )
    return (
        jnp.stack([diag_part, sub_part], axis=1),
        panel_part.reshape(panel_blocks * block, block),
    )


def step_block(diag, sub, panel_rows, inv_prev, sol_prev):
    low = jnp.dot(sub, inv_prev.T, precision=HIGH)
    inverse = invert_lower(jnp.linalg.cholesky(diag - jnp.dot(low, low.T, precision=HIGH)))
    solved = jnp.dot(inverse, panel_rows - jnp.dot(low, sol_prev, precision=HIGH), precision=HIGH)
    return (inverse, solved)


def run_blocks(blocks, panel, inv_prev, sol_prev):
    inv_prev, sol_prev = step_block(blocks[0, 0], blocks[0, 1], panel, inv_prev, sol_prev)
    pieces = [sol_prev]
    return (inv_prev, sol_prev, jnp.concatenate(pieces, axis=0))


def body(local_derivs, global_derivs, weights, first_block, bundle_count, trailing_block):
    block = global_derivs.shape[2] // 3
    slots = local_derivs.shape[0]
    live = (jnp.arange(slots, dtype=jnp.int32) < bundle_count[0]).astype(jnp.float32)
    stacked, panel_part = bundle_terms(
        local_derivs, global_derivs, weights, first_block, live, PBLK
    )
    n_rec = lax.axis_size("rec")
    n_row = lax.axis_size("row")
    rec_index = lax.axis_index("rec")
    identity = jnp.eye(block, dtype=jnp.float32)
    empty = jnp.zeros((block, block), jnp.float32)
    blocks_mine, panel_mine = (
        lax.psum_scatter(stacked, "rec", scatter_dimension=0, tiled=True),
        lax.psum_scatter(panel_part, "rec", scatter_dimension=0, tiled=True),
    )
    blocks_mine = lax.psum(blocks_mine, ("row", "col"))

    def one_round(turn, carry):
        inv_last, sol_last, _ = run_blocks(blocks_mine, panel_mine, carry[0], carry[1])
        inv_in, sol_in = shifted((inv_last, sol_last), "rec", 1)
        inv_in = jnp.where(rec_index == 0, identity, inv_in)
        return (inv_in, sol_in)

    inv_prev, sol_prev = lax.fori_loop(0, n_rec - 1, one_round, (identity, empty))
    _, _, solved = run_blocks(blocks_mine, panel_mine, inv_prev, sol_prev)
    solved_low = solved.astype(jnp.bfloat16)
    tile_rows = trailing_block.shape[0]
    tile_cols = trailing_block.shape[1]
    whole = lax.all_gather(solved_low, ("row", "col"), axis=1, tiled=True)
    span = whole.shape[0]
    grid = whole.reshape(span, n_rec, n_row, tile_rows)
    row_part = lax.dynamic_slice_in_dim(grid, lax.axis_index("row"), 1, 2).reshape(
        span, n_rec, tile_rows
    )
    col_part = lax.dynamic_slice_in_dim(whole, lax.axis_index("col") * tile_cols, tile_cols, 1)
    left = lax.all_to_all(row_part, "rec", split_axis=1, concat_axis=0, tiled=True).reshape(
        span * n_rec, tile_rows
    )
    right = lax.all_gather(col_part, "rec", axis=0, tiled=True)
    update = lax.dot_general(
        left, right, (((0,), (0,)), ((), ())), preferred_element_type=jnp.float32
    )
    return trailing_block - update


def solution(mesh):
    return jax.shard_map(
        body,
        mesh=mesh,
        in_specs=(
            P(("rec", "row", "col"), None, None),
            P(("rec", "row", "col"), None, None),
            P(("rec", "row", "col"), None),
            P(("rec", "row", "col")),
            P(("rec", "row", "col")),
            P(("rec", "row"), "col"),
        ),
        out_specs=P(("rec", "row"), "col"),
        check_vma=False,
    )
```

profile of v0, /device:TPU:10, one launch (start us, length us, event | category | flops | bytes accessed | tf_op | source)
XLA Modules:
  0.0 1233.5 jit_solution(695342394293087570)
XLA Ops:
  12.0 23.5 %custom-call.12 = f32[2,128,128]{2,1,0:T(8,128)S(1)} custom-call(f32[2,128,128]{2,1,0:T(8,128)S(1)} %fusion.16), custom_call_target="Cholesky" | custom-call | tf_op jit(solution)/shard_map/jit(cholesky)/cholesky | solution.py:41
  35.7 19.7 %custom-call.13 = f32[2,1,128,128]{2,3,1,0:T(8,128)S(1)} custom-call(f32[2,1,128,128]{3,2,1,0:T(8,128)S(1)} %select_bitcast_fusion), custom_call_target="InvertDiagBlocksLowerTriangular" | custom-call | tf_op jit(solution)/shard_map/triangular_solve | solution.py:21
  63.3 92.8 %reduce-scatter.3.cloned.1.call-done = f32[1,2,128,128]{2,3,1,0:T(8,128)} async-done(((f32[8,2,128,128]{2,3,1,0:T(8,128)}), f32[1,2,128,128]{2,3,1,0:T(8,128)}) %reduce-scatter.3.cloned.1.call-update) | async-done | bytes 131088 | tf_op jit(solution)/shard_map/reduce_scatter | solution.py:95
  156.2 90.6 %reduce-scatter.5.cloned.1.call-done = f32[128,128]{1,0:T(8,128)} async-done(((f32[1024,128]{1,0:T(8,128)}), f32[128,128]{1,0:T(8,128)}) %reduce-scatter.5.cloned.1.call-update) | async-done | bytes 65552 | tf_op jit(solution)/shard_map/reduce_scatter | solution.py:96
  246.8 436.3 %all-reduce.2.cloned.1.call-done = f32[1,2,128,128]{2,3,1,0:T(8,128)} async-done(((f32[1,2,128,128]{2,3,1,0:T(8,128)}), f32[1,2,128,128]{2,3,1,0:T(8,128)}) %all-reduce.2.cloned.1.call-update) | async-done | bytes 131088 | tf_op jit(solution)/shard_map/psum | solution.py:98
  683.1 295.6 %while.15 = (s32[]{:T(128)}, f32[128,128]{1,0:T(8,128)S(1)}, f32[128,128]{1,0:T(8,128)S(1)}, pred[]{:T(512)}, f32[1,2,128,128]{2,3,1,0:T(8,128)}, /*index=5*/f32[128,128]{1,0:T(8,128)}, s32[]{:T(128)}) while((s32[]{:T(128)}, f32[128,128]{1,0:T(8,128)S(1)}, f32[128,128]{1,0:T(8,128)S(1)}, pred[]{:T(512)}, ...), condition=%wide.region_8.11_spmd.clone, body=%wide.region_5.10_spmd.clone.sunk | while | flops 126091392 | bytes 2229408 | solution.py:106
  685.5 11.7 cholesky.183
  698.5 9.8 custom-call.18
  730.6 11.7 cholesky.183
  743.6 9.8 custom-call.18
  770.7 11.7 cholesky.183
  783.8 9.8 custom-call.18
  815.9 11.7 cholesky.183
  828.9 9.8 custom-call.18
  855.9 11.7 cholesky.183
  868.9 9.8 custom-call.18
  900.9 11.7 cholesky.183
  913.9 9.8 custom-call.18
  941.2 11.7 cholesky.183
  954.2 9.8 custom-call.18
  981.0 11.7 cholesky.103
  1006.1 147.7 %all-gather.3.cloned.1.call-done = bf16[128,8192]{1,0:T(8,128)(2,1)} async-done(((bf16[128,128]{1,0:T(8,128)(2,1)}), bf16[128,8192]{1,0:T(8,128)(2,1)}) %all-gather.3.cloned.1.call-update) | async-done | bytes 2097168 | tf_op jit(solution)/shard_map/all_gather | solution.py:111
  1160.2 29.9 %all_to_all.15 = bf16[128,8,256]{2,0,1:T(8,128)(2,1)S(1)} all-to-all(bf16[128,8,256]{2,0,1:T(8,128)(2,1)S(1)} %bitcast.111), channel_id=1, replica_groups=mesh['rec'=8,'row'=4,'col'=16] {'rec'}, dimensions={1} | all-to-all | bytes 1048576 | tf_op jit(solution)/shard_map/all_to_all | solution.py:118
  1190.1 34.4 %all-gather.5.cloned.1.call-done = bf16[1024,512]{1,0:T(8,128)(2,1)} async-done(((bf16[128,512]{1,0:T(8,128)(2,1)}), bf16[1024,512]{1,0:T(8,128)(2,1)}) %all-gather.5.cloned.1.call-update) | async-done | bytes 1048592 | tf_op jit(solution)/shard_map/all_gather | solution.py:121
  (167 shorter events, 181.6 us)
Async XLA Ops:
  6.5 5.3 copy-start.1
  6.5 149.6 %reduce-scatter.3.cloned.1.call-start = ((), (), s32[]{:S(2)}) async-start(), calls=%async_computation.3 | async-start | bytes 1179648 | tf_op jit(solution)/shard_map/reduce_scatter | solution.py:95
  61.1 185.7 %reduce-scatter.5.cloned.1.call-start = ((), (), s32[]{:S(2)}) async-start(), calls=%async_computation.5 | async-start | bytes 589824 | tf_op jit(solution)/shard_map/reduce_scatter | solution.py:96
  63.3 619.8 %all-reduce.2.cloned.1.call-start = ((), (), s32[]{:S(2)}) async-start(), calls=%async_computation.4 | async-start | bytes 262144 | tf_op jit(solution)/shard_map/psum | solution.py:98
  156.1 997.7 %all-gather.3.cloned.1.call-start = ((), (), s32[]{:S(2)}) async-start(), calls=%async_computation.6 | async-start | bytes 2129920 | tf_op jit(solution)/shard_map/all_gather | solution.py:111
  708.6 11.9 collective-permute-start
  717.2 11.0 collective-permute-start.1
  753.7 11.9 collective-permute-start
  757.4 11.0 collective-permute-start.1
  793.9 11.6 collective-permute-start
  802.5 11.0 collective-permute-start.1
  839.0 11.6 collective-permute-start
  842.4 11.1 collective-permute-start.1
  879.0 12.0 collective-permute-start
  887.5 11.0 collective-permute-start.1
  924.0 11.0 collective-permute-start
  927.9 11.0 collective-permute-start.1
  964.3 11.7 collective-permute-start
  967.7 11.0 collective-permute-start.1
  1006.1 218.4 %all-gather.5.cloned.1.call-start = ((), (), s32[]{:S(2)}) async-start(), calls=%async_computation.7 | async-start | bytes 1179648 | tf_op jit(solution)/shard_map/all_gather | solution.py:121
  1158.7 65.7 %copy-start = (f32[256,512]{1,0:T(8,128)S(1)}, f32[256,512]{1,0:T(8,128)}, u32[]{:S(2)}) copy-start(f32[256,512]{1,0:T(8,128)} %param.16) | copy-start | bytes 1572868
Sparse Core Ops, SparseCore 0:
  61.2 94.8 reduce-scatter.2
  160.6 86.2 reduce-scatter.4
  249.8 433.3 all-reduce.1
  1006.2 147.5 all-gather.2
  1156.9 67.5 all-gather.4
where the time goes:
time: 1240 us; the launch traced here: 1230 us
  waiting for transfers between devices  846 us (68%)
  other arithmetic  228 us (18%)
  starting transfers between devices  63.6 us (5%)
  matrix products  40.6 us (3%)
  blocking collectives  29.9 us (2%)
  between operations  14.1 us (1%)
    psum x1, waiting for transfers between devices, body(): blocks_mine = lax.psum(blocks_mine, ('row', 'col'))  436 us
    all_gather x1, waiting for transfers between devices, body(): whole = lax.all_gather(solved_low, ('row', 'col'), axis=1, tiled=True)  148 us
    another operation x19, other arithmetic, invert_lower(): return lax.linalg.triangular_solve(factor, eye, left_side=True, lower=True)  104 us
    another operation x25, other arithmetic, step_block(): jnp.linalg.cholesky(diag - jnp.dot(low, low.T, precision=HIGH))  99.1 us
    reduce_scatter x1, waiting for transfers between devices, body(): lax.psum_scatter(stacked, 'rec', scatter_dimension=0, tiled=True)  92.8 us
    reduce_scatter x1, waiting for transfers between devices, body(): lax.psum_scatter(panel_part, 'rec', scatter_dimension=0, tiled=True)  90.6 us
    ppermute x14, starting transfers between devices, shifted(): return lax.ppermute(shard, axis, pairs)  63.2 us
    ppermute x14, waiting for transfers between devices, shifted(): return lax.ppermute(shard, axis, pairs)  44.6 us
  transfers between devices with their start and end apart: 19, of which 14 were waited for; matrix products, arithmetic and copies ran while one was open for 1% of the time, Pallas kernels for 0%

commit v1 on v0

v1 whole, which is shorter than its diff:
```python
import functools

import jax
import jax.numpy as jnp
from jax import lax
from jax.experimental import pallas as pl
from jax.experimental.pallas import tpu as pltpu
from jax.sharding import PartitionSpec as P

HIGH = lax.Precision.HIGHEST
MESH = pl.DeviceIdType.MESH
BLK = 128
PBLK = 8
HALF = BLK // 2
F32 = jnp.float32
BF16 = jnp.bfloat16


def recip(x):
    r = pl.reciprocal(x, approx=True)
    r = r * (2.0 - x * r)
    return r * (2.0 - x * r)


def lane(x, at):
    return jnp.broadcast_to(x[:, at : at + 1], x.shape)


def row(x, at):
    return jnp.broadcast_to(x[at : at + 1, :], x.shape)


def strip_sweep(strips, j, base, sub, lan):
    inside = (lan >= base) & (lan < base + 8)
    panel = strips[j]
    others = [o for o in range(len(strips)) if o != j]
    cols = [lane(panel, base + k) for k in range(8)]
    outer = [[lane(strips[o], base + k) for o in others] for k in range(8)]
    x = jnp.where(inside, jnp.where(lan - base == sub, -1.0, 0.0), panel)
    for i in range(0, 8, 2):
        c0, c1 = cols[i], cols[i + 1]
        a, b, c = row(c0, i), row(c0, i + 1), row(c1, i + 1)
        rd = recip(a * c - b * b)
        first, second = sub == i, sub == i + 1
        ra, rb, rc = a * rd, b * rd, c * rd

        def step(v):
            p, q = row(v, i), row(v, i + 1)
            u = rc * p - rb * q
            w = ra * q - rb * p
            return jnp.where(first, u, jnp.where(second, w, v - c0 * u - c1 * w))

        cols = [step(v) if k > i + 1 else v for k, v in enumerate(cols)]
        x = step(x)
    rows = [row(x, k) for k in range(8)]
    new = list(strips)
    for at, o in enumerate(others):
        acc = jnp.where(inside, 0.0, strips[o])
        for k in range(8):
            acc = acc - outer[k][at] * rows[k]
        new[o] = acc
    new[j] = x
    return new


def minus_inverse(mats, width=2):
    n = mats[0].shape[0]
    h = 8 * width
    sub = lax.broadcasted_iota(jnp.int32, (8, n), 0)
    lan = lax.broadcasted_iota(jnp.int32, (8, n), 1)
    wide = lax.broadcasted_iota(jnp.int32, (n, n), 1)
    for low in range(0, n, h):
        panels = [[a[low + 8 * s : low + 8 * s + 8, :] for s in range(width)] for a in mats]
        for s in range(width):
            panels = [strip_sweep(p, s, low + 8 * s, sub, lan) for p in panels]
        out = []
        for a, p in zip(mats, panels):
            w = jnp.concatenate(p, axis=0)
            above = [jnp.zeros((low, n), F32)] if low else []
            below = [jnp.zeros((n - low - h, n), F32)] if low + h < n else []
            pad = jnp.concatenate(above + [w] + below, axis=0)
            keep = jnp.where((wide >= low) & (wide < low + h), 0.0, a)
            new = keep - jnp.dot(a, pad, precision=HIGH, preferred_element_type=F32)
            parts = ([new[:low]] if low else []) + [w] + ([new[low + h :]] if low + h < n else [])
            out.append(jnp.concatenate(parts, axis=0))
        mats = out
    return mats


def dot(a, b):
    return jnp.dot(a, b, precision=HIGH, preferred_element_type=F32)


def dot_t(a, b):
    return lax.dot_general(a, b, (((1,), (1,)), ((), ())), precision=HIGH, preferred_element_type=F32)


def t_dot(a, b, precision=HIGH):
    return lax.dot_general(
        a, b, (((0,), (0,)), ((), ())), precision=precision, preferred_element_type=F32
    )


def bundle_kernel(first_ref, count_ref, loc_ref, glo_ref, wts_ref, t_ref, p_ref):
    slots = loc_ref.shape[0]
    rows = loc_ref.shape[1]
    grams, crosses, panels = [], [], []
    for b in range(slots):
        columns = []
        for part in range(rows // BLK):
            w = jnp.sqrt(wts_ref[b : b + 1, part * BLK : part * BLK + BLK])
            column = jnp.transpose(jnp.broadcast_to(w, (8, BLK)))[:, 0:1]
            columns.append(column)
        root = jnp.concatenate(columns, axis=0)
        sl = (root * loc_ref[b].astype(F32)).astype(BF16)
        sg = (root * glo_ref[b].astype(F32)).astype(BF16)
        grams.append(t_dot(sl, sl, None))
        crosses.append(t_dot(sl, sg, None))
        panels.append(t_dot(sg[:, : 2 * BLK], sg, None))
    minus = minus_inverse(grams)
    reduced = []
    for b in range(slots):
        live = (b < count_ref[0]).astype(F32)
        fitted = dot(minus[b], crosses[b])
        reduced.append((panels[b] + t_dot(crosses[b][:, : 2 * BLK], fitted)) * live)
    for k in range(PBLK):
        diag = jnp.zeros((BLK, BLK), F32)
        below = jnp.zeros((BLK, BLK), F32)
        rhs = jnp.zeros((BLK, BLK), F32)
        for b in range(slots):
            first = (first_ref[b] == k).astype(F32)
            second = (first_ref[b] + 1 == k).astype(F32)
            r = reduced[b]
            if k < PBLK - 1:
                diag = diag + first * r[:BLK, :BLK]
                rhs = rhs + first * r[:BLK, 2 * BLK :]
            if k > 0:
                diag = diag + second * r[BLK:, BLK : 2 * BLK]
                below = below + second * r[BLK:, :BLK]
                rhs = rhs + second * r[BLK:, 2 * BLK :]
        t_ref[0, k] = diag.astype(BF16)
        t_ref[1, k] = below.astype(BF16)
        p_ref[k] = rhs.astype(BF16)


def device(x, h, l, z, c):
    return {"rec": x * 2 + h, "row": l, "col": z * 2 + c}


def remote(src, dst, send_sem, recv_sem, to):
    return pltpu.make_async_remote_copy(
        src_ref=src,
        dst_ref=dst,
        send_sem=send_sem,
        recv_sem=recv_sem,
        device_id=to,
        device_id_type=MESH,
    )


def loop(low, high, step):
    def one(at, carry):
        step(at)
        return carry

    lax.fori_loop(low, high, one, 0)


def exchange_kernel(
    t_in, p_in, t_out, left, right,
    tc, ts, tz1, ty1, tz2, ty2, tx, half2, half3, px, pa, pp, py, pc,
    s_tc, r_tc, s_z1, r_z1, s_y1, r_y1, s_z2, r_z2, s_y2, r_y2, s_tx, r_tx,
    s_z3, r_z3, s_y3, r_y3, s_f, r_f, s_px, r_px, s_py, r_py,
    s_rg, r_rg, s_lg, r_lg, s_ry, r_ry, s_rx, r_rx, s_lz, r_lz, s_lc, r_lc,
):
    rec, l, col = lax.axis_index("rec"), lax.axis_index("row"), lax.axis_index("col")
    x, h, z, c = rec // 2, rec % 2, col // 2, col % 2
    y = h * 4 + l
    me = device(x, h, l, z, c)
    pair = device(x, h, l, z, 1 - c)
    partner = device(x, 1 - h, l, z, c)

    def at_z(i):
        return device(x, h, l, i, c)

    def at_y(i):
        return device(x, i // 4, i % 4, z, c)

    def at_x(i):
        return device(i, h, l, z, c)

    mine = 2 * x + h
    right_source = z // 2 == l
    left_source = y == z
    right_z, right_c, right_j = 2 * l + z // 4, (z % 4) // 2, 2 * (z % 2) + c
    right_home = (right_z == z) & (right_c == c)
    right_to = device(x, h, l, right_z, right_c)
    left_home = (l == x) & (z == y)
    left_to = device(l, z // 4, z % 4, z, c)

    barrier = pltpu.get_barrier_semaphore()

    def greet(to):
        pl.semaphore_signal(barrier, inc=1, device_id=to, device_id_type=MESH)

    greet(pair)
    loop(1, 8, lambda d: greet(at_z((z + d) % 8)))
    loop(1, 8, lambda d: greet(at_y((y + d) % 8)))
    loop(1, 4, lambda d: greet(at_x((x + d) % 4)))

    @pl.when(right_source)
    def _():
        for j in range(4):
            from_z, from_c = 4 * (z % 2) + 2 * c + j // 2, j % 2

            @pl.when((from_z != z) | (from_c != c))
            def _():
                greet(device(x, h, l, from_z, from_c))

    @pl.when(left_source)
    def _():
        for k in range(8):

            @pl.when((k != mine) | (l != x))
            def _():
                greet(device(k // 2, k % 2, x, z, c))

    away = jnp.where(right_home, 0, 1) + jnp.where(left_home, 0, 1)
    pl.semaphore_wait(barrier, 18 + away)

    copy_tc = remote(t_in.at[1 - c], tc, s_tc, r_tc, pair)
    copy_tc.start()

    def panel_x(d):
        to = (x + d) % 4
        return remote(p_in.at[pl.ds(2 * to, 2)], px.at[d], s_px.at[d], r_px.at[d], at_x(to))

    loop(1, 4, lambda d: panel_x(d).start())

    copy_tc.wait_recv()

    def pair_sum(i):
        ts[i] = (t_in[c, i].astype(F32) + tc[i].astype(F32)).astype(BF16)

    loop(0, 8, pair_sum)

    def send_z1(d):
        to = (z + d) % 8
        return remote(ts.at[to, pl.ds(0, HALF)], tz1.at[d], s_z1.at[d], r_z1.at[d], at_z(to))

    def send_y1(d):
        to = (y + d) % 8
        return remote(ts.at[to, pl.ds(HALF, HALF)], ty1.at[d], s_y1.at[d], r_y1.at[d], at_y(to))

    def start_1(d):
        send_z1(d).start()
        send_y1(d).start()

    loop(1, 8, start_1)

    for d in range(1, 4):
        panel_x(d).wait_recv()
    for hh in range(2):
        total = p_in[2 * x + hh].astype(F32)
        for d in range(1, 4):
            total = total + px[d, hh].astype(F32)
        pa[hh] = total
    pp[...] = pa[1 - h].astype(BF16)
    copy_py = remote(pp, py, s_py, r_py, partner)
    copy_py.start()

    def wait_1(d):
        send_z1(d).wait_recv()
        send_y1(d).wait_recv()

    loop(1, 8, wait_1)
    sum_z = ts[z, 0:HALF].astype(F32)
    sum_y = ts[y, HALF:BLK].astype(F32)
    for d in range(1, 8):
        sum_z = sum_z + tz1[d].astype(F32)
        sum_y = sum_y + ty1[d].astype(F32)
    half2[0] = sum_z.astype(BF16)
    half2[1] = sum_y.astype(BF16)

    def send_y2(d):
        to = (y + d) % 8
        return remote(half2.at[0], ty2.at[d], s_y2.at[d], r_y2.at[d], at_y(to))

    def send_z2(d):
        to = (z + d) % 8
        return remote(half2.at[1], tz2.at[d], s_z2.at[d], r_z2.at[d], at_z(to))

    def start_2(d):
        send_y2(d).start()
        send_z2(d).start()

    loop(1, 8, start_2)

    copy_py.wait_recv()
    piece = (pa[h] + py[...].astype(F32)).astype(BF16)
    pc[...] = piece
    copy_rg = remote(pc, right.at[mine, right_j], s_rg, r_rg.at[right_j], right_to)
    copy_lg = remote(pc, left.at[c, mine], s_lg, r_lg.at[mine], left_to)

    @pl.when(right_home)
    def _():
        right[mine, right_j] = piece

    @pl.when(jnp.logical_not(right_home))
    def _():
        copy_rg.start()

    @pl.when(left_home)
    def _():
        left[c, mine] = piece

    @pl.when(jnp.logical_not(left_home))
    def _():
        copy_lg.start()

    def wait_2(d):
        send_y2(d).wait_recv()
        send_z2(d).wait_recv()

    loop(1, 8, wait_2)
    sum_z = half2[0].astype(F32)
    sum_y = half2[1].astype(F32)
    for d in range(1, 8):
        sum_z = sum_z + ty2[d].astype(F32)
        sum_y = sum_y + tz2[d].astype(F32)
    half3[0] = sum_z
    half3[1] = sum_y

    def send_tx(d):
        return remote(half3, tx.at[d], s_tx.at[d], r_tx.at[d], at_x((x + d) % 4))

    loop(1, 4, lambda d: send_tx(d).start())
    loop(1, 4, lambda d: send_tx(d).wait_recv())
    sum_z, sum_y = half3[0], half3[1]
    for d in range(1, 4):
        sum_z = sum_z + tx[d, 0]
        sum_y = sum_y + tx[d, 1]
    t_out[c, z, 0:HALF] = sum_z
    t_out[c, y, HALF:BLK] = sum_y

    def upper(cc, i):
        return t_out.at[cc, i, pl.ds(0, HALF)]

    def lower(cc, i):
        return t_out.at[cc, i, pl.ds(HALF, HALF)]

    def send_z3(d):
        return remote(upper(c, z), upper(c, z), s_z3.at[d], r_z3.at[d], at_z((z + d) % 8))

    def send_y3(d):
        return remote(lower(c, y), lower(c, y), s_y3.at[d], r_y3.at[d], at_y((y + d) % 8))

    def got_z3(d):
        i = (z + 8 - d) % 8
        return remote(upper(c, i), upper(c, i), s_z3.at[d], r_z3.at[d], at_z(i))

    def got_y3(d):
        i = (y + 8 - d) % 8
        return remote(lower(c, i), lower(c, i), s_y3.at[d], r_y3.at[d], at_y(i))

    def across_z(cc, i):
        return remote(upper(cc, i), upper(cc, i), s_f.at[i], r_f.at[i], pair)

    def across_y(cc, i):
        return remote(lower(cc, i), lower(cc, i), s_f.at[8 + i], r_f.at[8 + i], pair)

    def start_3(d):
        send_z3(d).start()
        send_y3(d).start()

    loop(1, 8, start_3)
    across_z(c, z).start()
    across_y(c, y).start()

    def right_y(d):
        return remote(right.at[mine], right.at[mine], s_ry.at[d], r_ry.at[h], at_y((y + d) % 8))

    def left_z(d):
        return remote(left.at[c], left.at[c], s_lz.at[d], r_lz, at_z((z + d) % 8))

    @pl.when(right_source)
    def _():
        for j in range(4):
            from_z, from_c = 4 * (z % 2) + 2 * c + j // 2, j % 2

            @pl.when((from_z != z) | (from_c != c))
            def _():
                remote(pc, right.at[mine, j], s_rg, r_rg.at[j], device(x, h, l, from_z, from_c)).wait_recv()

        loop(1, 8, lambda d: right_y(d).start())

    @pl.when(left_source)
    def _():
        for k in range(8):

            @pl.when((k != mine) | (l != x))
            def _():
                remote(pc, left.at[c, k], s_lg, r_lg.at[k], device(k // 2, k % 2, x, z, c)).wait_recv()

        loop(1, 8, lambda d: left_z(d).start())

    def arrived_3(d):
        got_z3(d).wait_recv()
        across_z(c, (z + 8 - d) % 8).start()
        got_y3(d).wait_recv()
        across_y(c, (y + 8 - d) % 8).start()

    loop(1, 8, arrived_3)

    def right_x(hh, d):
        block = right.at[2 * x + hh]
        at = hh * 4 + d
        return remote(block, block, s_rx.at[at], r_rx.at[at], at_x((x + d) % 4))

    for hh in range(2):
        source = 4 * hh + z // 2

        @pl.when(y != source)
        def _():
            block = right.at[2 * x + hh]
            remote(block, block, s_ry.at[0], r_ry.at[hh], at_y(source)).wait_recv()

        loop(1, 4, lambda d: right_x(hh, d).start())

    @pl.when(y != z)
    def _():
        remote(left.at[c], left.at[c], s_lz.at[0], r_lz, at_z(y)).wait_recv()

    copy_lc = remote(left.at[c], left.at[c], s_lc, r_lc, pair)
    copy_lc.start()

    def across(i):
        across_z(1 - c, i).wait_recv()
        across_y(1 - c, i).wait_recv()

    loop(0, 8, across)
    remote(left.at[1 - c], left.at[1 - c], s_lc, r_lc, pair).wait_recv()
    for hh in range(2):

        def got_x(d):
            i = (x + 4 - d) % 4
            block = right.at[2 * i + hh]
            remote(block, block, s_rx.at[hh * 4 + d], r_rx.at[hh * 4 + d], at_x(i)).wait_recv()

        loop(1, 4, got_x)

    copy_tc.wait_send()
    copy_py.wait_send()
    copy_lc.wait_send()

    @pl.when(jnp.logical_not(right_home))
    def _():
        copy_rg.wait_send()

    @pl.when(jnp.logical_not(left_home))
    def _():
        copy_lg.wait_send()

    def sent_7(d):
        send_z1(d).wait_send()
        send_y1(d).wait_send()
        send_z2(d).wait_send()
        send_y2(d).wait_send()
        send_z3(d).wait_send()
        send_y3(d).wait_send()

    loop(1, 8, sent_7)

    def sent_3(d):
        panel_x(d).wait_send()
        send_tx(d).wait_send()
        right_x(0, d).wait_send()
        right_x(1, d).wait_send()

    loop(1, 4, sent_3)

    def sent_8(i):
        across_z(c, i).wait_send()
        across_y(c, i).wait_send()

    loop(0, 8, sent_8)

    @pl.when(right_source)
    def _():
        loop(1, 8, lambda d: right_y(d).wait_send())

    @pl.when(left_source)
    def _():
        loop(1, 8, lambda d: left_z(d).wait_send())


def eliminate_kernel(t_ref, left_ref, right_ref, trail_ref, out_ref, p_ref):
    for k in range(PBLK):
        for i in range(2):
            p_ref[k, :, i * BLK : i * BLK + BLK] = left_ref[i, k].astype(F32)
        for j in range(4):
            p_ref[k, :, (2 + j) * BLK : (3 + j) * BLK] = right_ref[k, j].astype(F32)
    diag = [t_ref[0, k] for k in range(PBLK)]
    below = [None] + [t_ref[1, k] for k in range(1, PBLK)]
    out_ref[...] = trail_ref[...]

    def couple(gain, source, target):
        p_ref[target] = p_ref[target] + dot(gain, p_ref[source])

    def finish(k, minus):
        solved = dot(minus, p_ref[k, :, 2 * BLK :])
        out_ref[...] = out_ref[...] + t_dot(p_ref[k, :, : 2 * BLK], solved)

    n0, n2, n5, n7 = minus_inverse([diag[0], diag[2], diag[5], diag[7]])
    g01 = dot(below[1], n0)
    g21 = t_dot(below[2], n2)
    g23 = dot(below[3], n2)
    g54 = t_dot(below[5], n5)
    g56 = dot(below[6], n5)
    g76 = t_dot(below[7], n7)
    d1 = diag[1] + dot_t(g01, below[1]) + dot(g21, below[2])
    d6 = diag[6] + dot_t(g56, below[6]) + dot(g76, below[7])
    d3 = diag[3] + dot_t(g23, below[3])
    d4 = diag[4] + dot(g54, below[5])
    f31 = dot(g23, below[2])
    f64 = dot(g56, below[5])
    couple(g01, 0, 1)
    couple(g21, 2, 1)
    couple(g23, 2, 3)
    couple(g54, 5, 4)
    couple(g56, 5, 6)
    couple(g76, 7, 6)
    n1, n6 = minus_inverse([d1, d6])
    g13 = dot(f31, n1)
    g64 = t_dot(f64, n6)
    d3 = d3 + dot_t(g13, f31)
    d4 = d4 + dot(g64, f64)
    couple(g13, 1, 3)
    couple(g64, 6, 4)
    (n3,) = minus_inverse([d3])
    g34 = dot(below[4], n3)
    d4 = d4 + dot_t(g34, below[4])
    couple(g34, 3, 4)
    (n4,) = minus_inverse([d4])
    for k, minus in enumerate((n0, n1, n2, n3, n4, n5, n6, n7)):
        finish(k, minus)


def body(local_derivs, global_derivs, weights, first_block, bundle_count, trailing_block):
    vmem = pl.BlockSpec(memory_space=pltpu.VMEM)
    smem = pl.BlockSpec(memory_space=pltpu.SMEM)
    block = (BLK, BLK)
    shape = jax.ShapeDtypeStruct
    tri, panel = pl.pallas_call(
        bundle_kernel,
        name="bundles",
        in_specs=[smem, smem, vmem, vmem, vmem],
        out_specs=[vmem, vmem],
        out_shape=[shape((2, PBLK) + block, BF16), shape((PBLK,) + block, BF16)],
    )(first_block, bundle_count, local_derivs, global_derivs, weights)
    dma = pltpu.SemaphoreType.DMA
    half = (HALF, BLK)
    sems = (
        [dma, dma]
        + [dma((8,))] * 8
        + [dma((4,))] * 2
        + [dma((8,))] * 4
        + [dma((16,))] * 2
        + [dma((4,))] * 2
        + [dma, dma]
        + [dma, dma((4,)), dma, dma((8,))]
        + [dma((8,)), dma((2,)), dma((8,)), dma((8,))]
        + [dma((8,)), dma, dma, dma]
    )
    tri, left, right = pl.pallas_call(
        exchange_kernel,
        name="exchange",
        in_specs=[vmem, vmem],
        out_specs=[vmem, vmem, vmem],
        out_shape=[
            shape((2, PBLK) + block, F32),
            shape((2, PBLK) + block, BF16),
            shape((PBLK, 4) + block, BF16),
        ],
        scratch_shapes=[
            pltpu.VMEM((PBLK,) + block, BF16),
            pltpu.VMEM((PBLK,) + block, BF16),
            pltpu.VMEM((8,) + half, BF16),
            pltpu.VMEM((8,) + half, BF16),
            pltpu.VMEM((8,) + half, BF16),
            pltpu.VMEM((8,) + half, BF16),
            pltpu.VMEM((4, 2) + half, F32),
            pltpu.VMEM((2,) + half, BF16),
            pltpu.VMEM((2,) + half, F32),
            pltpu.VMEM((4, 2) + block, BF16),
            pltpu.VMEM((2,) + block, F32),
            pltpu.VMEM(block, BF16),
            pltpu.VMEM(block, BF16),
            pltpu.VMEM(block, BF16),
        ]
        + sems,
        compiler_params=pltpu.CompilerParams(collective_id=0, has_side_effects=True),
    )(tri, panel)
    return pl.pallas_call(
        eliminate_kernel,
        name="eliminate",
        in_specs=[vmem] * 4,
        out_specs=vmem,
        out_shape=shape(trailing_block.shape, F32),
        scratch_shapes=[pltpu.VMEM((PBLK, BLK, 6 * BLK), F32)],
    )(tri, left, right, trailing_block)


def solution(mesh):
    return jax.shard_map(
        body,
        mesh=mesh,
        in_specs=(
            P(("rec", "row", "col"), None, None),
            P(("rec", "row", "col"), None, None),
            P(("rec", "row", "col"), None),
            P(("rec", "row", "col")),
            P(("rec", "row", "col")),
            P(("rec", "row"), "col"),
        ),
        out_specs=P(("rec", "row"), "col"),
        check_vma=False,
    )
```

time: 1240 us -> 113 us (0.09)
  the two profiles are of different devices: /device:TPU:10 before, /device:TPU:32 now
where the time goes in v1:
time: 113 us
  Pallas kernels  112 us (99%)
    pallas_call x1, Pallas kernels, body(): pl.pallas_call(exchange_kernel, name='exchange', in_specs=[vmem, vmem], o...  69.1 us
    pallas_call x1, Pallas kernels, body(): pl.pallas_call(eliminate_kernel, name='eliminate', in_specs=[vmem] * 4, o...  34 us
    pallas_call x1, Pallas kernels, body(): pl.pallas_call(bundle_kernel, name='bundles', in_specs=[smem, smem, vmem,...  9.42 us

profile of v1, /device:TPU:32, one launch (start us, length us, event | category | flops | bytes accessed | tf_op | source)
XLA Modules:
  0.0 113.1 jit_solution(4444359634206774332)
XLA Ops:
  0.7 9.4 %bundles.1 = (bf16[2,8,128,128]{3,2,1,0:T(8,128)(2,1)}, bf16[8,128,128]{2,1,0:T(8,128)(2,1)}) custom-call(s32[2]{0:T(128)} %first_ref.1, s32[1]{0:T(128)S(6)} %copy.7.count_ref, bf16[2,256,128]{2,1,0:T(8,128)(2,1)} %loc_ref.1, bf16[2,256,384]{2,1,0:T(8,128)(2,1)} %glo_ref.1, f32[2,256]{1,0:T(2,128)} %wts_ref.1), custom_call_target="tpu_custom_call" | custom-call | tf_op jit(solution)/shard_map/bundles/pallas_call | solution.py:554
  10.1 69.1 %exchange.1 = (f32[2,8,128,128]{3,2,1,0:T(8,128)}, bf16[2,8,128,128]{3,2,1,0:T(8,128)(2,1)}, bf16[8,4,128,128]{3,2,1,0:T(8,128)(2,1)}) custom-call(bf16[2,8,128,128]{3,2,1,0:T(8,128)(2,1)} %get-tuple-element.10.t_in, bf16[8,128,128]{2,1,0:T(8,128)(2,1)} %get-tuple-element.11.p_in), custom_call_target="tpu_custom_call" | custom-call | tf_op jit(solution)/shard_map/exchange/pallas_call | solution.py:575
  79.1 34.0 %eliminate.1 = f32[256,512]{1,0:T(8,128)} custom-call(f32[2,8,128,128]{3,2,1,0:T(8,128)} %get-tuple-element.12.t_ref, bf16[2,8,128,128]{3,2,1,0:T(8,128)(2,1)} %get-tuple-element.13.left_ref, bf16[8,4,128,128]{3,2,1,0:T(8,128)(2,1)} %get-tuple-element.14.right_ref, f32[256,512]{1,0:T(8,128)} %trail_ref.1), custom_call_target="tpu_custom_call" | custom-call | tf_op jit(solution)/shard_map/eliminate/pallas_call | solution.py:604

commit v2 on v1

v2 whole, which is shorter than its diff:
```python
import functools

import jax
import jax.numpy as jnp
from jax import lax
from jax.experimental import pallas as pl
from jax.experimental.pallas import tpu as pltpu
from jax.sharding import PartitionSpec as P

HIGH = lax.Precision.HIGHEST
MESH = pl.DeviceIdType.MESH
BLK = 128
PBLK = 8
HALF = BLK // 2
STRIPS = 4
F32 = jnp.float32
BF16 = jnp.bfloat16


def recip(x):
    r = pl.reciprocal(x, approx=True)
    return r * (2.0 - x * r)


def row(v, i):
    return jnp.broadcast_to(v[..., i:i + 1, :], v.shape)


def tree(v):
    while v.shape[0] > 1:
        half = v.shape[0] // 2
        v = v[:half] + v[half:]
    return v[0]


def strip_sweep(strips, j, base, sub, lan):
    inside = (lan >= base) & (lan < base + 8)
    panel = strips[j]
    shape = panel.shape

    def columns(s):
        return [jnp.broadcast_to(s[:, :, base + k:base + k + 1], shape) for k in range(8)]

    others = [o for o in range(len(strips)) if o != j]
    state = columns(panel)
    outer = [columns(strips[o]) for o in others]
    state = jnp.stack(state + [jnp.where(inside, jnp.where(lan - base == sub, -1.0, 0.0), panel)])
    for i in range(0, 8, 2):
        c0, c1 = state[0], state[1]
        a, b, c = row(c0, i), row(c0, i + 1), row(c1, i + 1)
        rd = recip(a * c - b * b)
        v = state[2:]
        p, q = row(v, i), row(v, i + 1)
        u = (c * rd) * p - (b * rd) * q
        w = (a * rd) * q - (b * rd) * p
        state = jnp.where(sub == i, u, jnp.where(sub == i + 1, w, v - (c0 * u + c1 * w)))
    x = state[0]
    rows = jnp.stack([row(x, k) for k in range(8)])
    new = list(strips)
    for at, o in enumerate(others):
        new[o] = jnp.where(inside, 0.0, strips[o]) - tree(jnp.stack(outer[at]) * rows)
    new[j] = x
    return new


def minus_inverse(mats):
    n = mats[0].shape[0]
    h = 8 * STRIPS
    sub = lax.broadcasted_iota(jnp.int32, (8, n), 0)
    lan = lax.broadcasted_iota(jnp.int32, (8, n), 1)
    wide = lax.broadcasted_iota(jnp.int32, (n, n), 1)
    for low in range(0, n, h):
        strips = [jnp.stack([a[low + 8 * s:low + 8 * s + 8, :] for a in mats]) for s in range(STRIPS)]
        for s in range(STRIPS):
            strips = strip_sweep(strips, s, low + 8 * s, sub, lan)
        out = []
        for m, a in enumerate(mats):
            w = jnp.concatenate([s[m] for s in strips], axis=0)
            above = [jnp.zeros((low, n), F32)] if low else []
            below = [jnp.zeros((n - low - h, n), F32)] if low + h < n else []
            pad = jnp.concatenate(above + [w] + below, axis=0)
            keep = jnp.where((wide >= low) & (wide < low + h), 0.0, a)
            new = keep - jnp.dot(a, pad, precision=HIGH, preferred_element_type=F32)
            parts = ([new[:low]] if low else []) + [w] + ([new[low + h:]] if low + h < n else [])
            out.append(jnp.concatenate(parts, axis=0))
        mats = out
    return mats


def dot(a, b):
    return jnp.dot(a, b, precision=HIGH, preferred_element_type=F32)


def dot_t(a, b):
    return lax.dot_general(a, b, (((1,), (1,)), ((), ())), precision=HIGH, preferred_element_type=F32)


def t_dot(a, b, precision=HIGH):
    return lax.dot_general(
        a, b, (((0,), (0,)), ((), ())), precision=precision, preferred_element_type=F32
    )


def bundle_terms(first_ref, count_ref, loc_ref, glo_ref, wts_ref, t_ref, p_ref):
    slots = loc_ref.shape[0]
    rows = loc_ref.shape[1]
    grams, crosses, panels = [], [], []
    for b in range(slots):
        columns = []
        for part in range(rows // BLK):
            w = jnp.sqrt(wts_ref[b : b + 1, part * BLK : part * BLK + BLK])
            column = jnp.transpose(jnp.broadcast_to(w, (8, BLK)))[:, 0:1]
            columns.append(column)
        root = jnp.concatenate(columns, axis=0)
        sl = (root * loc_ref[b].astype(F32)).astype(BF16)
        sg = (root * glo_ref[b].astype(F32)).astype(BF16)
        grams.append(t_dot(sl, sl, None))
        crosses.append(t_dot(sl, sg, None))
        panels.append(t_dot(sg[:, : 2 * BLK], sg, None))
    minus = minus_inverse(grams)
    reduced = []
    for b in range(slots):
        live = (b < count_ref[0]).astype(F32)
        fitted = dot(minus[b], crosses[b])
        reduced.append((panels[b] + t_dot(crosses[b][:, : 2 * BLK], fitted)) * live)
    for k in range(PBLK):
        diag = jnp.zeros((BLK, BLK), F32)
        below = jnp.zeros((BLK, BLK), F32)
        rhs = jnp.zeros((BLK, BLK), F32)
        for b in range(slots):
            first = (first_ref[b] == k).astype(F32)
            second = (first_ref[b] + 1 == k).astype(F32)
            r = reduced[b]
            if k < PBLK - 1:
                diag = diag + first * r[:BLK, :BLK]
                rhs = rhs + first * r[:BLK, 2 * BLK :]
            if k > 0:
                diag = diag + second * r[BLK:, BLK : 2 * BLK]
                below = below + second * r[BLK:, :BLK]
                rhs = rhs + second * r[BLK:, 2 * BLK :]
        t_ref[0, k] = diag.astype(BF16)
        t_ref[1, k] = below.astype(BF16)
        p_ref[k] = rhs.astype(BF16)


def eliminate(t_ref, left_ref, right_ref, out_ref, p_ref, between, panel_ready):
    diag = [t_ref[0, k] for k in range(PBLK)]
    below = [None] + [t_ref[1, k] for k in range(1, PBLK)]

    def couple(gain, source, target):
        p_ref[target] = p_ref[target] + dot(gain, p_ref[source])

    n0, n2, n5, n7 = minus_inverse([diag[0], diag[2], diag[5], diag[7]])
    between()
    g01 = dot(below[1], n0)
    g21 = t_dot(below[2], n2)
    g23 = dot(below[3], n2)
    g54 = t_dot(below[5], n5)
    g56 = dot(below[6], n5)
    g76 = t_dot(below[7], n7)
    d1 = diag[1] + dot_t(g01, below[1]) + dot(g21, below[2])
    d6 = diag[6] + dot_t(g56, below[6]) + dot(g76, below[7])
    d3 = diag[3] + dot_t(g23, below[3])
    d4 = diag[4] + dot(g54, below[5])
    f31 = dot(g23, below[2])
    f64 = dot(g56, below[5])
    n1, n6 = minus_inverse([d1, d6])
    g13 = dot(f31, n1)
    g64 = t_dot(f64, n6)
    d3 = d3 + dot_t(g13, f31)
    d4 = d4 + dot(g64, f64)
    (n3,) = minus_inverse([d3])
    g34 = dot(below[4], n3)
    d4 = d4 + dot_t(g34, below[4])
    panel_ready()
    for k in range(PBLK):
        for i in range(2):
            p_ref[k, :, i * BLK : i * BLK + BLK] = left_ref[i, k].astype(F32)
        for j in range(4):
            p_ref[k, :, (2 + j) * BLK : (3 + j) * BLK] = right_ref[k, j].astype(F32)
    couple(g01, 0, 1)
    couple(g21, 2, 1)
    couple(g23, 2, 3)
    couple(g54, 5, 4)
    couple(g56, 5, 6)
    couple(g76, 7, 6)
    couple(g13, 1, 3)
    couple(g64, 6, 4)
    couple(g34, 3, 4)
    (n4,) = minus_inverse([d4])
    total = None
    for k, minus in ((0, n0), (1, n1), (2, n2), (3, n3), (5, n5), (6, n6), (7, n7), (4, n4)):
        solved = dot(minus, p_ref[k, :, 2 * BLK :])
        part = t_dot(p_ref[k, :, : 2 * BLK], solved)
        total = part if total is None else total + part
    out_ref[...] = total


def device(x, h, l, z, c):
    return {"rec": x * 2 + h, "row": l, "col": z * 2 + c}


def remote(src, dst, send_sem, recv_sem, to):
    return pltpu.make_async_remote_copy(
        src_ref=src,
        dst_ref=dst,
        send_sem=send_sem,
        recv_sem=recv_sem,
        device_id=to,
        device_id_type=MESH,
    )


def loop(low, high, step):
    def one(at, carry):
        step(at)
        return carry

    lax.fori_loop(low, high, one, 0)


def main_kernel(
    first, count, loc, glo, wts, out,
    t_in, p_in, t_out, left, right, solve, tc, ts, tz1, ty1, tz2, ty2, tx, half2, half3, px, pa, pp, py, pc,
    s_tc, r_tc, s_z1, r_z1, s_y1, r_y1, s_z2, r_z2, s_y2, r_y2, s_tx, r_tx,
    s_z3, r_z3, s_y3, r_y3, s_f, r_f, s_px, r_px, s_py, r_py,
    s_rg, r_rg, s_lg, r_lg, s_ry, r_ry, s_rx, r_rx, s_lz, r_lz, s_lc, r_lc,
):
    rec, l, col = lax.axis_index("rec"), lax.axis_index("row"), lax.axis_index("col")
    x, h, z, c = rec // 2, rec % 2, col // 2, col % 2
    y = h * 4 + l
    me = device(x, h, l, z, c)
    pair = device(x, h, l, z, 1 - c)
    partner = device(x, 1 - h, l, z, c)

    def at_z(i):
        return device(x, h, l, i, c)

    def at_y(i):
        return device(x, i // 4, i % 4, z, c)

    def at_x(i):
        return device(i, h, l, z, c)

    mine = 2 * x + h
    right_source = z // 2 == l
    left_source = y == z
    right_z, right_c, right_j = 2 * l + z // 4, (z % 4) // 2, 2 * (z % 2) + c
    right_home = (right_z == z) & (right_c == c)
    right_to = device(x, h, l, right_z, right_c)
    left_home = (l == x) & (z == y)
    left_to = device(l, z // 4, z % 4, z, c)

    barrier = pltpu.get_barrier_semaphore()

    def greet(to):
        pl.semaphore_signal(barrier, inc=1, device_id=to, device_id_type=MESH)

    greet(pair)
    loop(1, 8, lambda d: greet(at_z((z + d) % 8)))
    loop(1, 8, lambda d: greet(at_y((y + d) % 8)))
    loop(1, 4, lambda d: greet(at_x((x + d) % 4)))

    @pl.when(right_source)
    def _():
        for j in range(4):
            from_z, from_c = 4 * (z % 2) + 2 * c + j // 2, j % 2

            @pl.when((from_z != z) | (from_c != c))
            def _():
                greet(device(x, h, l, from_z, from_c))

    @pl.when(left_source)
    def _():
        for k in range(8):

            @pl.when((k != mine) | (l != x))
            def _():
                greet(device(k // 2, k % 2, x, z, c))

    bundle_terms(first, count, loc, glo, wts, t_in, p_in)
    away = jnp.where(right_home, 0, 1) + jnp.where(left_home, 0, 1)
    pl.semaphore_wait(barrier, 18 + away)

    copy_tc = remote(t_in.at[1 - c], tc, s_tc, r_tc, pair)
    copy_tc.start()

    def panel_x(d):
        to = (x + d) % 4
        return remote(p_in.at[pl.ds(2 * to, 2)], px.at[d], s_px.at[d], r_px.at[d], at_x(to))

    loop(1, 4, lambda d: panel_x(d).start())

    copy_tc.wait_recv()

    def pair_sum(i):
        ts[i] = (t_in[c, i].astype(F32) + tc[i].astype(F32)).astype(BF16)

    loop(0, 8, pair_sum)

    def send_z1(d):
        to = (z + d) % 8
        return remote(ts.at[to, pl.ds(0, HALF)], tz1.at[d], s_z1.at[d], r_z1.at[d], at_z(to))

    def send_y1(d):
        to = (y + d) % 8
        return remote(ts.at[to, pl.ds(HALF, HALF)], ty1.at[d], s_y1.at[d], r_y1.at[d], at_y(to))

    def start_1(d):
        send_z1(d).start()
        send_y1(d).start()

    loop(1, 8, start_1)

    for d in range(1, 4):
        panel_x(d).wait_recv()
    for hh in range(2):
        total = p_in[2 * x + hh].astype(F32)
        for d in range(1, 4):
            total = total + px[d, hh].astype(F32)
        pa[hh] = total
    pp[...] = pa[1 - h].astype(BF16)
    copy_py = remote(pp, py, s_py, r_py, partner)
    copy_py.start()

    def wait_1(d):
        send_z1(d).wait_recv()
        send_y1(d).wait_recv()

    loop(1, 8, wait_1)
    sum_z = ts[z, 0:HALF].astype(F32)
    sum_y = ts[y, HALF:BLK].astype(F32)
    for d in range(1, 8):
        sum_z = sum_z + tz1[d].astype(F32)
        sum_y = sum_y + ty1[d].astype(F32)
    half2[0] = sum_z.astype(BF16)
    half2[1] = sum_y.astype(BF16)

    def send_y2(d):
        to = (y + d) % 8
        return remote(half2.at[0], ty2.at[d], s_y2.at[d], r_y2.at[d], at_y(to))

    def send_z2(d):
        to = (z + d) % 8
        return remote(half2.at[1], tz2.at[d], s_z2.at[d], r_z2.at[d], at_z(to))

    def start_2(d):
        send_y2(d).start()
        send_z2(d).start()

    loop(1, 8, start_2)

    copy_py.wait_recv()
    piece = (pa[h] + py[...].astype(F32)).astype(BF16)
    pc[...] = piece
    copy_rg = remote(pc, right.at[mine, right_j], s_rg, r_rg.at[right_j], right_to)
    copy_lg = remote(pc, left.at[c, mine], s_lg, r_lg.at[mine], left_to)

    @pl.when(right_home)
    def _():
        right[mine, right_j] = piece

    @pl.when(jnp.logical_not(right_home))
    def _():
        copy_rg.start()

    @pl.when(left_home)
    def _():
        left[c, mine] = piece

    @pl.when(jnp.logical_not(left_home))
    def _():
        copy_lg.start()

    def wait_2(d):
        send_y2(d).wait_recv()
        send_z2(d).wait_recv()

    loop(1, 8, wait_2)
    sum_z = half2[0].astype(F32)
    sum_y = half2[1].astype(F32)
    for d in range(1, 8):
        sum_z = sum_z + ty2[d].astype(F32)
        sum_y = sum_y + tz2[d].astype(F32)
    half3[0] = sum_z
    half3[1] = sum_y

    def send_tx(d):
        return remote(half3, tx.at[d], s_tx.at[d], r_tx.at[d], at_x((x + d) % 4))

    loop(1, 4, lambda d: send_tx(d).start())
    loop(1, 4, lambda d: send_tx(d).wait_recv())
    sum_z, sum_y = half3[0], half3[1]
    for d in range(1, 4):
        sum_z = sum_z + tx[d, 0]
        sum_y = sum_y + tx[d, 1]
    t_out[c, z, 0:HALF] = sum_z
    t_out[c, y, HALF:BLK] = sum_y

    def upper(cc, i):
        return t_out.at[cc, i, pl.ds(0, HALF)]

    def lower(cc, i):
        return t_out.at[cc, i, pl.ds(HALF, HALF)]

    def send_z3(d):
        return remote(upper(c, z), upper(c, z), s_z3.at[d], r_z3.at[d], at_z((z + d) % 8))

    def send_y3(d):
        return remote(lower(c, y), lower(c, y), s_y3.at[d], r_y3.at[d], at_y((y + d) % 8))

    def got_z3(d):
        i = (z + 8 - d) % 8
        return remote(upper(c, i), upper(c, i), s_z3.at[d], r_z3.at[d], at_z(i))

    def got_y3(d):
        i = (y + 8 - d) % 8
        return remote(lower(c, i), lower(c, i), s_y3.at[d], r_y3.at[d], at_y(i))

    def across_z(cc, i):
        return remote(upper(cc, i), upper(cc, i), s_f.at[i], r_f.at[i], pair)

    def across_y(cc, i):
        return remote(lower(cc, i), lower(cc, i), s_f.at[8 + i], r_f.at[8 + i], pair)

    def start_3(d):
        send_z3(d).start()
        send_y3(d).start()

    loop(1, 8, start_3)
    across_z(c, z).start()
    across_y(c, y).start()

    def right_y(d):
        return remote(right.at[mine], right.at[mine], s_ry.at[d], r_ry.at[h], at_y((y + d) % 8))

    def left_z(d):
        return remote(left.at[c], left.at[c], s_lz.at[d], r_lz, at_z((z + d) % 8))

    @pl.when(right_source)
    def _():
        for j in range(4):
            from_z, from_c = 4 * (z % 2) + 2 * c + j // 2, j % 2

            @pl.when((from_z != z) | (from_c != c))
            def _():
                remote(pc, right.at[mine, j], s_rg, r_rg.at[j], device(x, h, l, from_z, from_c)).wait_recv()

        loop(1, 8, lambda d: right_y(d).start())

    @pl.when(left_source)
    def _():
        for k in range(8):

            @pl.when((k != mine) | (l != x))
            def _():
                remote(pc, left.at[c, k], s_lg, r_lg.at[k], device(k // 2, k % 2, x, z, c)).wait_recv()

        loop(1, 8, lambda d: left_z(d).start())

    def arrived_3(d):
        got_z3(d).wait_recv()
        across_z(c, (z + 8 - d) % 8).start()
        got_y3(d).wait_recv()
        across_y(c, (y + 8 - d) % 8).start()

    loop(1, 8, arrived_3)

    def across(i):
        across_z(1 - c, i).wait_recv()
        across_y(1 - c, i).wait_recv()

    loop(0, 8, across)

    def right_x(hh, d):
        block = right.at[2 * x + hh]
        at = hh * 4 + d
        return remote(block, block, s_rx.at[at], r_rx.at[at], at_x((x + d) % 4))

    copy_lc = remote(left.at[c], left.at[c], s_lc, r_lc, pair)

    def pass_on():
        for hh in range(2):
            source = 4 * hh + z // 2

            @pl.when(y != source)
            def _():
                block = right.at[2 * x + hh]
                remote(block, block, s_ry.at[0], r_ry.at[hh], at_y(source)).wait_recv()

            loop(1, 4, lambda d: right_x(hh, d).start())

        @pl.when(y != z)
        def _():
            remote(left.at[c], left.at[c], s_lz.at[0], r_lz, at_z(y)).wait_recv()

        copy_lc.start()

    def panel_ready():
        remote(left.at[1 - c], left.at[1 - c], s_lc, r_lc, pair).wait_recv()
        for hh in range(2):

            def got_x(d):
                i = (x + 4 - d) % 4
                block = right.at[2 * i + hh]
                at = hh * 4 + d
                remote(block, block, s_rx.at[at], r_rx.at[at], at_x(i)).wait_recv()

            loop(1, 4, got_x)

    eliminate(t_out, left, right, out, solve, pass_on, panel_ready)

    copy_tc.wait_send()
    copy_py.wait_send()
    copy_lc.wait_send()

    @pl.when(jnp.logical_not(right_home))
    def _():
        copy_rg.wait_send()

    @pl.when(jnp.logical_not(left_home))
    def _():
        copy_lg.wait_send()

    def sent_7(d):
        send_z1(d).wait_send()
        send_y1(d).wait_send()
        send_z2(d).wait_send()
        send_y2(d).wait_send()
        send_z3(d).wait_send()
        send_y3(d).wait_send()

    loop(1, 8, sent_7)

    def sent_3(d):
        panel_x(d).wait_send()
        send_tx(d).wait_send()
        right_x(0, d).wait_send()
        right_x(1, d).wait_send()

    loop(1, 4, sent_3)

    def sent_8(i):
        across_z(c, i).wait_send()
        across_y(c, i).wait_send()

    loop(0, 8, sent_8)

    @pl.when(right_source)
    def _():
        loop(1, 8, lambda d: right_y(d).wait_send())

    @pl.when(left_source)
    def _():
        loop(1, 8, lambda d: left_z(d).wait_send())


def body(local_derivs, global_derivs, weights, first_block, bundle_count, trailing_block):
    vmem = pl.BlockSpec(memory_space=pltpu.VMEM)
    smem = pl.BlockSpec(memory_space=pltpu.SMEM)
    block = (BLK, BLK)
    shape = jax.ShapeDtypeStruct
    dma = pltpu.SemaphoreType.DMA
    half = (HALF, BLK)
    sems = (
        [dma, dma]
        + [dma((8,))] * 8
        + [dma((4,))] * 2
        + [dma((8,))] * 4
        + [dma((16,))] * 2
        + [dma((4,))] * 2
        + [dma, dma]
        + [dma, dma((4,)), dma, dma((8,))]
        + [dma((8,)), dma((2,)), dma((8,)), dma((8,))]
        + [dma((8,)), dma, dma, dma]
    )
    delta = pl.pallas_call(
        main_kernel,
        name="normal",
        in_specs=[smem, smem, vmem, vmem, vmem],
        out_specs=vmem,
        out_shape=shape(trailing_block.shape, F32),
        scratch_shapes=[
            pltpu.VMEM((2, PBLK) + block, BF16),
            pltpu.VMEM((PBLK,) + block, BF16),
            pltpu.VMEM((2, PBLK) + block, F32),
            pltpu.VMEM((2, PBLK) + block, BF16),
            pltpu.VMEM((PBLK, 4) + block, BF16),
            pltpu.VMEM((PBLK, BLK, 6 * BLK), F32),
            pltpu.VMEM((PBLK,) + block, BF16),
            pltpu.VMEM((PBLK,) + block, BF16),
            pltpu.VMEM((8,) + half, BF16),
            pltpu.VMEM((8,) + half, BF16),
            pltpu.VMEM((8,) + half, BF16),
            pltpu.VMEM((8,) + half, BF16),
            pltpu.VMEM((4, 2) + half, F32),
            pltpu.VMEM((2,) + half, BF16),
            pltpu.VMEM((2,) + half, F32),
            pltpu.VMEM((4, 2) + block, BF16),
            pltpu.VMEM((2,) + block, F32),
            pltpu.VMEM(block, BF16),
            pltpu.VMEM(block, BF16),
            pltpu.VMEM(block, BF16),
        ]
        + sems,
        compiler_params=pltpu.CompilerParams(collective_id=0, has_side_effects=True),
    )(first_block, bundle_count, local_derivs, global_derivs, weights)
    return trailing_block + delta


def solution(mesh):
    return jax.shard_map(
        body,
        mesh=mesh,
        in_specs=(
            P(("rec", "row", "col"), None, None),
            P(("rec", "row", "col"), None, None),
            P(("rec", "row", "col"), None),
            P(("rec", "row", "col")),
            P(("rec", "row", "col")),
            P(("rec", "row"), "col"),
        ),
        out_specs=P(("rec", "row"), "col"),
        check_vma=False,
    )
```

time: 113 us -> 95.9 us (0.85)
  the two profiles are of different devices: /device:TPU:32 before, /device:TPU:9 now
where the time goes in v2:
time: 95.9 us; the launch traced here: 95.7 us
  Pallas kernels  93.2 us (97%)
  other arithmetic  1.91 us (2%)
    pallas_call x1, Pallas kernels, body(): pl.pallas_call(main_kernel, name='normal', in_specs=[smem, smem, vmem, vm...  93.2 us

profile of v2, /device:TPU:9, one launch (start us, length us, event | category | flops | bytes accessed | tf_op | source)
XLA Modules:
  0.0 95.7 jit_solution(2274385879729529275)
XLA Ops:
  0.7 0.0 copy-start
  0.7 93.2 %normal.1 = f32[256,512]{1,0:T(8,128)} custom-call(s32[2]{0:T(128)} %first.1, s32[1]{0:T(128)S(6)} %copy.7.count, bf16[2,256,128]{2,1,0:T(8,128)(2,1)} %loc.1, bf16[2,256,384]{2,1,0:T(8,128)(2,1)} %glo.1, f32[2,256]{1,0:T(2,128)} %wts.1), custom_call_target="tpu_custom_call" | custom-call | tf_op jit(solution)/shard_map/normal/pallas_call | solution.py:577
  93.8 0.0 copy-done
  93.8 1.9 %add.3 = f32[256,512]{1,0:T(8,128)} add(f32[256,512]{1,0:T(8,128)S(1)} %copy-done, f32[256,512]{1,0:T(8,128)} %normal.1) | non-fusion elementwise | flops 131072 | bytes 1572864 | tf_op jit(solution)/shard_map/add | solution.py:608
Async XLA Ops:
  0.7 93.2 %copy-start = (f32[256,512]{1,0:T(8,128)S(1)}, f32[256,512]{1,0:T(8,128)}, u32[]{:S(2)}) copy-start(f32[256,512]{1,0:T(8,128)} %param.11) | copy-start | bytes 1572868

commit v3 on v2

--- a/solution.py
+++ b/solution.py
@@ -65,6 +65,14 @@
 
 def minus_inverse(mats):
     n = mats[0].shape[0]
+    eye = lax.broadcasted_iota(jnp.int32, (n, n), 0) == lax.broadcasted_iota(jnp.int32, (n, n), 1)
+    scales = []
+    for a in mats:
+        only = jnp.where(eye, a, 0.0)
+        down = lax.rsqrt(jnp.sum(only, axis=1, keepdims=True))
+        across = lax.rsqrt(jnp.sum(only, axis=0, keepdims=True))
+        scales.append((down, across))
+    mats = [a * down * across for a, (down, across) in zip(mats, scales)]
     h = 8 * STRIPS
     sub = lax.broadcasted_iota(jnp.int32, (8, n), 0)
     lan = lax.broadcasted_iota(jnp.int32, (8, n), 1)
@@ -84,116 +92,156 @@
             parts = ([new[:low]] if low else []) + [w] + ([new[low + h:]] if low + h < n else [])
             out.append(jnp.concatenate(parts, axis=0))
         mats = out
-    return mats
-
-
-def dot(a, b):
-    return jnp.dot(a, b, precision=HIGH, preferred_element_type=F32)
-
-
-def dot_t(a, b):
-    return lax.dot_general(a, b, (((1,), (1,)), ((), ())), precision=HIGH, preferred_element_type=F32)
-
-
-def t_dot(a, b, precision=HIGH):
-    return lax.dot_general(
-        a, b, (((0,), (0,)), ((), ())), precision=precision, preferred_element_type=F32
-    )
-
-
-def bundle_terms(first_ref, count_ref, loc_ref, glo_ref, wts_ref, t_ref, p_ref):
-    slots = loc_ref.shape[0]
-    rows = loc_ref.shape[1]
-    grams, crosses, panels = [], [], []
-    for b in range(slots):
+    return [a * down * across for a, (down, across) in zip(mats, scales)]
+
+
+def contract(a, b, da, db):
+    return lax.dot_general(a, b, (((da,), (db,)), ((), ())), preferred_element_type=F32)
+
+
+def split(a):
+    if a.dtype == BF16:
+        return a, None
+    high = a.astype(BF16)
+    return high, (a - high.astype(F32)).astype(BF16)
+
+
+def product(a, b, da=1, db=0):
+    (ah, al), (bh, bl) = a, b
+    total = contract(ah, bh, da, db)
+    if bl is not None:
+        total = total + contract(ah, bl, da, db)
+    if al is not None:
+        total = total + contract(al, bh, da, db)
+    return total
+
+
+def bundle_grams(loc_ref, glo_ref, wts_ref):
+    grams = []
+    for b in range(loc_ref.shape[0]):
         columns = []
-        for part in range(rows // BLK):
+        for part in range(loc_ref.shape[1] // BLK):
             w = jnp.sqrt(wts_ref[b : b + 1, part * BLK : part * BLK + BLK])
-            column = jnp.transpose(jnp.broadcast_to(w, (8, BLK)))[:, 0:1]
-            columns.append(column)
+            columns.append(jnp.transpose(jnp.broadcast_to(w, (8, BLK)))[:, 0:1])
         root = jnp.concatenate(columns, axis=0)
         sl = (root * loc_ref[b].astype(F32)).astype(BF16)
         sg = (root * glo_ref[b].astype(F32)).astype(BF16)
-        grams.append(t_dot(sl, sl, None))
-        crosses.append(t_dot(sl, sg, None))
-        panels.append(t_dot(sg[:, : 2 * BLK], sg, None))
-    minus = minus_inverse(grams)
+        pair = sg[:, : 2 * BLK]
+        grams.append(
+            (
+                contract(sl, sl, 0, 0),
+                split(contract(sl, sg, 0, 0)),
+                contract(pair, pair, 0, 0),
+                contract(sg[:, 2 * BLK :], pair, 0, 0),
+            )
+        )
+    return grams
+
+
+def flags(first_ref, count_ref, b, k):
+    live = (b < count_ref[0]).astype(F32)
+    first = (first_ref[b] == k).astype(F32) * live
+    second = (first_ref[b] + 1 == k).astype(F32) * live
+    return first, second
+
+
+def bundle_blocks(first_ref, count_ref, grams, fitted, t_ref):
     reduced = []
-    for b in range(slots):
-        live = (b < count_ref[0]).astype(F32)
-        fitted = dot(minus[b], crosses[b])
-        reduced.append((panels[b] + t_dot(crosses[b][:, : 2 * BLK], fitted)) * live)
+    for (_, cross, pair, _), fit in zip(grams, fitted):
+        two = tuple(v[:, : 2 * BLK] for v in cross)
+        reduced.append(pair + product(two, fit, 0, 0))
     for k in range(PBLK):
         diag = jnp.zeros((BLK, BLK), F32)
         below = jnp.zeros((BLK, BLK), F32)
-        rhs = jnp.zeros((BLK, BLK), F32)
-        for b in range(slots):
-            first = (first_ref[b] == k).astype(F32)
-            second = (first_ref[b] + 1 == k).astype(F32)
-            r = reduced[b]
+        for b, r in enumerate(reduced):
+            first, second = flags(first_ref, count_ref, b, k)
             if k < PBLK - 1:
                 diag = diag + first * r[:BLK, :BLK]
-                rhs = rhs + first * r[:BLK, 2 * BLK :]
             if k > 0:
-                diag = diag + second * r[BLK:, BLK : 2 * BLK]
+                diag = diag + second * r[BLK:, BLK:]
                 below = below + second * r[BLK:, :BLK]
-                rhs = rhs + second * r[BLK:, 2 * BLK :]
         t_ref[0, k] = diag.astype(BF16)
         t_ref[1, k] = below.astype(BF16)
+
+
+def bundle_panel(first_ref, count_ref, grams, fitted, p_ref):
+    reduced = []
+    for (_, cross, _, side), fit in zip(grams, fitted):
+        third = tuple(v[:, 2 * BLK :] for v in cross)
+        reduced.append(side + product(third, fit, 0, 0))
+    for k in range(PBLK):
+        rhs = jnp.zeros((BLK, BLK), F32)
+        for b, r in enumerate(reduced):
+            first, second = flags(first_ref, count_ref, b, k)
+            if k < PBLK - 1:
+                rhs = rhs + first * r[:, :BLK]
+            if k > 0:
+                rhs = rhs + second * r[:, BLK:]
         p_ref[k] = rhs.astype(BF16)
 
 
-def eliminate(t_ref, left_ref, right_ref, out_ref, p_ref, between, panel_ready):
+def eliminate(t_ref, left_ref, right_ref, out_ref, between, panel_ready):
     diag = [t_ref[0, k] for k in range(PBLK)]
-    below = [None] + [t_ref[1, k] for k in range(1, PBLK)]
-
-    def couple(gain, source, target):
-        p_ref[target] = p_ref[target] + dot(gain, p_ref[source])
-
-    n0, n2, n5, n7 = minus_inverse([diag[0], diag[2], diag[5], diag[7]])
+    below = [None] + [split(t_ref[1, k]) for k in range(1, PBLK)]
+
+    n0, n2, n5, n7 = [split(n) for n in minus_inverse([diag[0], diag[2], diag[5], diag[7]])]
     between()
-    g01 = dot(below[1], n0)
-    g21 = t_dot(below[2], n2)
-    g23 = dot(below[3], n2)
-    g54 = t_dot(below[5], n5)
-    g56 = dot(below[6], n5)
-    g76 = t_dot(below[7], n7)
-    d1 = diag[1] + dot_t(g01, below[1]) + dot(g21, below[2])
-    d6 = diag[6] + dot_t(g56, below[6]) + dot(g76, below[7])
-    d3 = diag[3] + dot_t(g23, below[3])
-    d4 = diag[4] + dot(g54, below[5])
-    f31 = dot(g23, below[2])
-    f64 = dot(g56, below[5])
-    n1, n6 = minus_inverse([d1, d6])
-    g13 = dot(f31, n1)
-    g64 = t_dot(f64, n6)
-    d3 = d3 + dot_t(g13, f31)
-    d4 = d4 + dot(g64, f64)
-    (n3,) = minus_inverse([d3])
-    g34 = dot(below[4], n3)
-    d4 = d4 + dot_t(g34, below[4])
+    g01 = split(product(below[1], n0))
+    g21 = split(product(below[2], n2, 0, 0))
+    g23 = split(product(below[3], n2))
+    g54 = split(product(below[5], n5, 0, 0))
+    g56 = split(product(below[6], n5))
+    g76 = split(product(below[7], n7, 0, 0))
+    d1 = diag[1] + product(g01, below[1], 1, 1) + product(g21, below[2])
+    d6 = diag[6] + product(g56, below[6], 1, 1) + product(g76, below[7])
+    d3 = diag[3] + product(g23, below[3], 1, 1)
+    d4 = diag[4] + product(g54, below[5])
+    f31 = split(product(g23, below[2]))
+    f64 = split(product(g56, below[5]))
+    n1, n6 = [split(n) for n in minus_inverse([d1, d6])]
+    g13 = split(product(f31, n1))
+    g64 = split(product(f64, n6, 0, 0))
+    d3 = d3 + product(g13, f31, 1, 1)
+    d4 = d4 + product(g64, f64)
+    n3 = split(minus_inverse([d3])[0])
+    g34 = split(product(below[4], n3))
+    d4 = d4 + product(g34, below[4], 1, 1)
     panel_ready()
-    for k in range(PBLK):
-        for i in range(2):
-            p_ref[k, :, i * BLK : i * BLK + BLK] = left_ref[i, k].astype(F32)
-        for j in range(4):
-            p_ref[k, :, (2 + j) * BLK : (3 + j) * BLK] = right_ref[k, j].astype(F32)
-    couple(g01, 0, 1)
-    couple(g21, 2, 1)
-    couple(g23, 2, 3)
-    couple(g54, 5, 4)
-    couple(g56, 5, 6)
-    couple(g76, 7, 6)
-    couple(g13, 1, 3)
-    couple(g64, 6, 4)
-    couple(g34, 3, 4)
-    (n4,) = minus_inverse([d4])
-    total = None
-    for k, minus in ((0, n0), (1, n1), (2, n2), (3, n3), (5, n5), (6, n6), (7, n7), (4, n4)):
-        solved = dot(minus, p_ref[k, :, 2 * BLK :])
-        part = t_dot(p_ref[k, :, : 2 * BLK], solved)
-        total = part if total is None else total + part
-    out_ref[...] = total
+
+    def panel(k):
+        parts = [left_ref[i, k] for i in range(2)] + [right_ref[k, j] for j in range(4)]
+        return jnp.concatenate(parts, axis=0)
+
+    def onto(k, *pairs):
+        total = panel(k).astype(F32)
+        for source, gain in pairs:
+            total = total + product(source, gain, 1, 1)
+        return split(total)
+
+    p0, p2, p5, p7 = [split(panel(k)) for k in (0, 2, 5, 7)]
+    p1 = onto(1, (p0, g01), (p2, g21))
+    p6 = onto(6, (p5, g56), (p7, g76))
+    p3 = onto(3, (p2, g23), (p1, g13))
+    p4 = onto(4, (p5, g54), (p6, g64), (p3, g34))
+
+    def sides(p):
+        cut = 2 * BLK
+        return [tuple(None if v is None else v[at] for v in p) for at in (slice(0, cut), slice(cut, None))]
+
+    def update(blocks):
+        lefts, rights = [], []
+        for p, n in blocks:
+            one, other = sides(p)
+            low = jnp.zeros_like(one[0]) if one[1] is None else one[1]
+            lefts.append((one[0], low))
+            rights.append(split(product(other, n)))
+        high_l, low_l = [jnp.concatenate(v, axis=1) for v in zip(*lefts)]
+        high_r, low_r = [jnp.concatenate(v, axis=1) for v in zip(*rights)]
+        return product((high_l, low_l), (high_r, low_r), 1, 1)
+
+    early = update([(p0, n0), (p1, n1), (p2, n2), (p3, n3), (p5, n5), (p6, n6)])
+    n4 = split(minus_inverse([d4])[0])
+    out_ref[...] = early + update([(p4, n4), (p7, n7)])
 
 
 def device(x, h, l, z, c):
@@ -221,7 +269,7 @@
 
 def main_kernel(
     first, count, loc, glo, wts, out,
-    t_in, p_in, t_out, left, right, solve, tc, ts, tz1, ty1, tz2, ty2, tx, half2, half3, px, pa, pp, py, pc,
+    t_in, p_in, t_out, left, right, tc, ts, tz1, ty1, tz2, ty2, tx, half2, half3, px, pa, pp, py, pc,
     s_tc, r_tc, s_z1, r_z1, s_y1, r_y1, s_z2, r_z2, s_y2, r_y2, s_tx, r_tx,
     s_z3, r_z3, s_y3, r_y3, s_f, r_f, s_px, r_px, s_py, r_py,
     s_rg, r_rg, s_lg, r_lg, s_ry, r_ry, s_rx, r_rx, s_lz, r_lz, s_lc, r_lc,
@@ -278,12 +326,21 @@
             def _():
                 greet(device(k // 2, k % 2, x, z, c))
 
-    bundle_terms(first, count, loc, glo, wts, t_in, p_in)
+    grams = bundle_grams(loc, glo, wts)
+    minus = [split(n) for n in minus_inverse([g[0] for g in grams])]
+    fitted = [
+        split(product(n, tuple(v[:, : 2 * BLK] for v in g[1]))) for n, g in zip(minus, grams)
+    ]
+    bundle_blocks(first, count, grams, fitted, t_in)
     away = jnp.where(right_home, 0, 1) + jnp.where(left_home, 0, 1)
     pl.semaphore_wait(barrier, 18 + away)
 
-    copy_tc = remote(t_in.at[1 - c], tc, s_tc, r_tc, pair)
-    copy_tc.start()
+    def across_tc(i):
+        return remote(t_in.at[1 - c, i], tc.at[i], s_tc.at[i], r_tc.at[i], pair)
+
+    loop(0, 8, lambda i: across_tc(i).start())
+
+    bundle_panel(first, count, grams, fitted, p_in)
 
     def panel_x(d):
         to = (x + d) % 4
@@ -291,13 +348,6 @@
 
     loop(1, 4, lambda d: panel_x(d).start())
 
-    copy_tc.wait_recv()
-
-    def pair_sum(i):
-        ts[i] = (t_in[c, i].astype(F32) + tc[i].astype(F32)).astype(BF16)
-
-    loop(0, 8, pair_sum)
-
     def send_z1(d):
         to = (z + d) % 8
         return remote(ts.at[to, pl.ds(0, HALF)], tz1.at[d], s_z1.at[d], r_z1.at[d], at_z(to))
@@ -306,11 +356,19 @@
         to = (y + d) % 8
         return remote(ts.at[to, pl.ds(HALF, HALF)], ty1.at[d], s_y1.at[d], r_y1.at[d], at_y(to))
 
-    def start_1(d):
-        send_z1(d).start()
-        send_y1(d).start()
-
-    loop(1, 8, start_1)
+    def start_1(i):
+        across_tc(i).wait_recv()
+        ts[i] = (t_in[c, i].astype(F32) + tc[i].astype(F32)).astype(BF16)
+
+        @pl.when(i != z)
+        def _():
+            send_z1((i + 8 - z) % 8).start()
+
+        @pl.when(i != y)
+        def _():
+            send_y1((i + 8 - y) % 8).start()
+
+    loop(0, 8, start_1)
 
     for d in range(1, 4):
         panel_x(d).wait_recv()
@@ -382,18 +440,18 @@
     for d in range(1, 8):
         sum_z = sum_z + ty2[d].astype(F32)
         sum_y = sum_y + tz2[d].astype(F32)
-    half3[0] = sum_z
-    half3[1] = sum_y
+    half3[0] = sum_z.astype(BF16)
+    half3[1] = sum_y.astype(BF16)
 
     def send_tx(d):
         return remote(half3, tx.at[d], s_tx.at[d], r_tx.at[d], at_x((x + d) % 4))
 
     loop(1, 4, lambda d: send_tx(d).start())
     loop(1, 4, lambda d: send_tx(d).wait_recv())
-    sum_z, sum_y = half3[0], half3[1]
+    sum_z, sum_y = half3[0].astype(F32), half3[1].astype(F32)
     for d in range(1, 4):
-        sum_z = sum_z + tx[d, 0]
-        sum_y = sum_y + tx[d, 1]
+        sum_z = sum_z + tx[d, 0].astype(F32)
+        sum_y = sum_y + tx[d, 1].astype(F32)
     t_out[c, z, 0:HALF] = sum_z
     t_out[c, y, HALF:BLK] = sum_y
 
@@ -508,9 +566,9 @@
 
             loop(1, 4, got_x)
 
-    eliminate(t_out, left, right, out, solve, pass_on, panel_ready)
-
-    copy_tc.wait_send()
+    eliminate(t_out, left, right, out, pass_on, panel_ready)
+
+    loop(0, 8, lambda i: across_tc(i).wait_send())
     copy_py.wait_send()
     copy_lc.wait_send()
 
@@ -563,8 +621,7 @@
     dma = pltpu.SemaphoreType.DMA
     half = (HALF, BLK)
     sems = (
-        [dma, dma]
-        + [dma((8,))] * 8
+        [dma((8,))] * 10
         + [dma((4,))] * 2
         + [dma((8,))] * 4
         + [dma((16,))] * 2
@@ -586,16 +643,15 @@
             pltpu.VMEM((2, PBLK) + block, F32),
             pltpu.VMEM((2, PBLK) + block, BF16),
             pltpu.VMEM((PBLK, 4) + block, BF16),
-            pltpu.VMEM((PBLK, BLK, 6 * BLK), F32),
             pltpu.VMEM((PBLK,) + block, BF16),
             pltpu.VMEM((PBLK,) + block, BF16),
             pltpu.VMEM((8,) + half, BF16),
             pltpu.VMEM((8,) + half, BF16),
             pltpu.VMEM((8,) + half, BF16),
             pltpu.VMEM((8,) + half, BF16),
-            pltpu.VMEM((4, 2) + half, F32),
+            pltpu.VMEM((4, 2) + half, BF16),
             pltpu.VMEM((2,) + half, BF16),
-            pltpu.VMEM((2,) + half, F32),
+            pltpu.VMEM((2,) + half, BF16),
             pltpu.VMEM((4, 2) + block, BF16),
             pltpu.VMEM((2,) + block, F32),
             pltpu.VMEM(block, BF16),

time: 95.9 us -> 86.7 us (0.904)
  the two profiles are of different devices: /device:TPU:9 before, /device:TPU:32 now
where the time goes in v3:
time: 86.7 us; the launch traced here: 85 us
  Pallas kernels  82.4 us (95%)
  other arithmetic  1.91 us (2%)
    pallas_call x1, Pallas kernels, body(): pl.pallas_call(main_kernel, name='normal', in_specs=[smem, smem, vmem, vm...  82.4 us
    add x1, other arithmetic, body(): return trailing_block + delta  1.91 us

profile of v3, /device:TPU:32, one launch (start us, length us, event | category | flops | bytes accessed | tf_op | source)
XLA Modules:
  0.0 85.0 jit_solution(14665958708548474695)
XLA Ops:
  0.7 0.0 copy-start
  0.7 82.4 %normal.1 = f32[256,512]{1,0:T(8,128)} custom-call(s32[2]{0:T(128)} %first.1, s32[1]{0:T(128)S(6)} %copy.7.count, bf16[2,256,128]{2,1,0:T(8,128)(2,1)} %loc.1, bf16[2,256,384]{2,1,0:T(8,128)(2,1)} %glo.1, f32[2,256]{1,0:T(2,128)} %wts.1), custom_call_target="tpu_custom_call" | custom-call | tf_op jit(solution)/shard_map/normal/pallas_call | solution.py:634
  83.1 0.0 copy-done
  83.1 1.9 %add.3 = f32[256,512]{1,0:T(8,128)} add(f32[256,512]{1,0:T(8,128)S(1)} %copy-done, f32[256,512]{1,0:T(8,128)} %normal.1) | non-fusion elementwise | flops 131072 | bytes 1572864 | tf_op jit(solution)/shard_map/add | solution.py:664
Async XLA Ops:
  0.7 82.4 %copy-start = (f32[256,512]{1,0:T(8,128)S(1)}, f32[256,512]{1,0:T(8,128)}, u32[]{:S(2)}) copy-start(f32[256,512]{1,0:T(8,128)} %param.11) | copy-start | bytes 1572868

commit v4 on v3

--- a/solution.py
+++ b/solution.py
@@ -291,13 +291,13 @@
         return device(i, h, l, z, c)
 
     mine = 2 * x + h
-    right_source = z // 2 == l
-    left_source = y == z
     right_z, right_c, right_j = 2 * l + z // 4, (z % 4) // 2, 2 * (z % 2) + c
-    right_home = (right_z == z) & (right_c == c)
-    right_to = device(x, h, l, right_z, right_c)
-    left_home = (l == x) & (z == y)
-    left_to = device(l, z // 4, z % 4, z, c)
+    right_home = (right_j == l) & (right_z == z) & (right_c == c)
+    right_to = device(x, h, right_j, right_z, right_c)
+    right_from = device(x, h, z // 2, 4 * (z % 2) + 2 * c + l // 2, l % 2)
+    left_home = (l == x) & (z == y) & (mine == z)
+    left_to = device(l, z // 4, z % 4, mine, c)
+    left_from = device(z // 2, z % 2, x, y, c)
 
     barrier = pltpu.get_barrier_semaphore()
 
@@ -309,22 +309,13 @@
     loop(1, 8, lambda d: greet(at_y((y + d) % 8)))
     loop(1, 4, lambda d: greet(at_x((x + d) % 4)))
 
-    @pl.when(right_source)
-    def _():
-        for j in range(4):
-            from_z, from_c = 4 * (z % 2) + 2 * c + j // 2, j % 2
-
-            @pl.when((from_z != z) | (from_c != c))
-            def _():
-                greet(device(x, h, l, from_z, from_c))
-
-    @pl.when(left_source)
-    def _():
-        for k in range(8):
-
-            @pl.when((k != mine) | (l != x))
-            def _():
-                greet(device(k // 2, k % 2, x, z, c))
+    @pl.when(jnp.logical_not(right_home))
+    def _():
+        greet(right_from)
+
+    @pl.when(jnp.logical_not(left_home))
+    def _():
+        greet(left_from)
 
     grams = bundle_grams(loc, glo, wts)
     minus = [split(n) for n in minus_inverse([g[0] for g in grams])]
@@ -411,8 +402,8 @@
     copy_py.wait_recv()
     piece = (pa[h] + py[...].astype(F32)).astype(BF16)
     pc[...] = piece
-    copy_rg = remote(pc, right.at[mine, right_j], s_rg, r_rg.at[right_j], right_to)
-    copy_lg = remote(pc, left.at[c, mine], s_lg, r_lg.at[mine], left_to)
+    copy_rg = remote(pc, right.at[mine, right_j], s_rg, r_rg, right_to)
+    copy_lg = remote(pc, left.at[c, mine], s_lg, r_lg, left_to)
 
     @pl.when(right_home)
     def _():
@@ -490,31 +481,34 @@
     across_y(c, y).start()
 
     def right_y(d):
-        return remote(right.at[mine], right.at[mine], s_ry.at[d], r_ry.at[h], at_y((y + d) % 8))
+        piece_at = right.at[mine, l]
+        return remote(piece_at, piece_at, s_ry.at[d], r_ry.at[d], at_y((y + d) % 8))
+
+    def got_right_y(d):
+        i = (y + 8 - d) % 8
+        piece_at = right.at[2 * x + i // 4, i % 4]
+        return remote(piece_at, piece_at, s_ry.at[d], r_ry.at[d], at_y(i))
 
     def left_z(d):
-        return remote(left.at[c], left.at[c], s_lz.at[d], r_lz, at_z((z + d) % 8))
-
-    @pl.when(right_source)
-    def _():
-        for j in range(4):
-            from_z, from_c = 4 * (z % 2) + 2 * c + j // 2, j % 2
-
-            @pl.when((from_z != z) | (from_c != c))
-            def _():
-                remote(pc, right.at[mine, j], s_rg, r_rg.at[j], device(x, h, l, from_z, from_c)).wait_recv()
-
-        loop(1, 8, lambda d: right_y(d).start())
-
-    @pl.when(left_source)
-    def _():
-        for k in range(8):
-
-            @pl.when((k != mine) | (l != x))
-            def _():
-                remote(pc, left.at[c, k], s_lg, r_lg.at[k], device(k // 2, k % 2, x, z, c)).wait_recv()
-
-        loop(1, 8, lambda d: left_z(d).start())
+        piece_at = left.at[c, z]
+        return remote(piece_at, piece_at, s_lz.at[d], r_lz.at[d], at_z((z + d) % 8))
+
+    def got_left_z(d):
+        i = (z + 8 - d) % 8
+        piece_at = left.at[c, i]
+        return remote(piece_at, piece_at, s_lz.at[d], r_lz.at[d], at_z(i))
+
+    @pl.when(jnp.logical_not(right_home))
+    def _():
+        remote(pc, right.at[mine, l], s_rg, r_rg, right_from).wait_recv()
+
+    loop(1, 8, lambda d: right_y(d).start())
+
+    @pl.when(jnp.logical_not(left_home))
+    def _():
+        remote(pc, left.at[c, z], s_lg, r_lg, left_from).wait_recv()
+
+    loop(1, 8, lambda d: left_z(d).start())
 
     def arrived_3(d):
         got_z3(d).wait_recv()
@@ -538,20 +532,10 @@
     copy_lc = remote(left.at[c], left.at[c], s_lc, r_lc, pair)
 
     def pass_on():
+        loop(1, 8, lambda d: got_right_y(d).wait_recv())
         for hh in range(2):
-            source = 4 * hh + z // 2
-
-            @pl.when(y != source)
-            def _():
-                block = right.at[2 * x + hh]
-                remote(block, block, s_ry.at[0], r_ry.at[hh], at_y(source)).wait_recv()
-
             loop(1, 4, lambda d: right_x(hh, d).start())
-
-        @pl.when(y != z)
-        def _():
-            remote(left.at[c], left.at[c], s_lz.at[0], r_lz, at_z(y)).wait_recv()
-
+        loop(1, 8, lambda d: got_left_z(d).wait_recv())
         copy_lc.start()
 
     def panel_ready():
@@ -604,13 +588,11 @@
 
     loop(0, 8, sent_8)
 
-    @pl.when(right_source)
-    def _():
-        loop(1, 8, lambda d: right_y(d).wait_send())
-
-    @pl.when(left_source)
-    def _():
-        loop(1, 8, lambda d: left_z(d).wait_send())
+    def sent_panel(d):
+        right_y(d).wait_send()
+        left_z(d).wait_send()
+
+    loop(1, 8, sent_panel)
 
 
 def body(local_derivs, global_derivs, weights, first_block, bundle_count, trailing_block):
@@ -627,9 +609,9 @@
         + [dma((16,))] * 2
         + [dma((4,))] * 2
         + [dma, dma]
-        + [dma, dma((4,)), dma, dma((8,))]
-        + [dma((8,)), dma((2,)), dma((8,)), dma((8,))]
-        + [dma((8,)), dma, dma, dma]
+        + [dma, dma, dma, dma]
+        + [dma((8,))] * 6
+        + [dma, dma]
     )
     delta = pl.pallas_call(
         main_kernel,

time: 86.7 us -> 83.1 us (0.958)
  the two profiles are of different devices: /device:TPU:32 before, /device:TPU:1 now
where the time goes in v4:
time: 83.1 us; the launch traced here: 82.9 us
  Pallas kernels  80.3 us (97%)
  other arithmetic  1.91 us (2%)
    pallas_call x1, Pallas kernels, body(): pl.pallas_call(main_kernel, name='normal', in_specs=[smem, smem, vmem, vm...  80.3 us
    add x1, other arithmetic, body(): return trailing_block + delta  1.91 us

profile of v4, /device:TPU:1, one launch (start us, length us, event | category | flops | bytes accessed | tf_op | source)
XLA Modules:
  0.0 82.9 jit_solution(9347911606723129262)
XLA Ops:
  0.7 0.0 copy-start
  0.7 80.3 %normal.1 = f32[256,512]{1,0:T(8,128)} custom-call(s32[2]{0:T(128)} %first.1, s32[1]{0:T(128)S(6)} %copy.7.count, bf16[2,256,128]{2,1,0:T(8,128)(2,1)} %loc.1, bf16[2,256,384]{2,1,0:T(8,128)(2,1)} %glo.1, f32[2,256]{1,0:T(2,128)} %wts.1), custom_call_target="tpu_custom_call" | custom-call | tf_op jit(solution)/shard_map/normal/pallas_call | solution.py:616
  81.0 0.0 copy-done
  81.0 1.9 %add.3 = f32[256,512]{1,0:T(8,128)} add(f32[256,512]{1,0:T(8,128)S(1)} %copy-done, f32[256,512]{1,0:T(8,128)} %normal.1) | non-fusion elementwise | flops 131072 | bytes 1572864 | tf_op jit(solution)/shard_map/add | solution.py:646
Async XLA Ops:
  0.7 80.3 %copy-start = (f32[256,512]{1,0:T(8,128)S(1)}, f32[256,512]{1,0:T(8,128)}, u32[]{:S(2)}) copy-start(f32[256,512]{1,0:T(8,128)} %param.11) | copy-start | bytes 1572868
